TPU v7x, 32 devices: a whole 2x2x4 slice. The times are simulated.
32 devices in a mesh: groups: 2 (over y), ctx: 4 (over z), head: 2 (over x), tp: 2 (over core).
Axes of the slice: x: 2, y: 2, z: 4, core: 2. Of those that a mesh axis runs over, the one named last changes fastest.
Arguments:
- queries: bfloat16 [32, 2048, 128], P(('head', 'tp'), ('groups', 'ctx')), parts along dimension 1, may hold values from -80 to 80
- stretch_keys: bfloat16 [8, 2048, 128], P(('head', 'tp'), ('groups', 'ctx')), parts along dimension 1, may hold values from -120 to 120
- stretch_values: bfloat16 [8, 2048, 128], P(('head', 'tp'), ('groups', 'ctx')), parts along dimension 1, may hold values from -6 to 6
- cache_keys: bfloat16 [8, 32768, 128], P(('head', 'tp'), ('groups', 'ctx')), parts along dimension 1, may hold values from -6 to 6
- cache_values: bfloat16 [8, 32768, 128], P(('head', 'tp'), ('groups', 'ctx')), parts along dimension 1, may hold values from -6 to 6
- block_picks: int32 [4, 8, 16], P('groups'), parts along dimension 0, may hold values from 0 to 31, as said below
- block_table: int32 [64], P('groups'), parts along dimension 0, may hold values from 0 to 31, as said below
Outputs:
- attended: bfloat16 [32, 2048, 128], P(('head', 'tp'), ('groups', 'ctx')), parts along dimension 1
There are 2 independent parts, one for each index of `groups`. A program takes and returns all parts, laid end to end along the dimension named above; each array names one. Nothing has to cross between parts.
Inputs may be any that keep to these rules, and one draw needn't show every extreme that they name: `block_picks`: for each query block and KV head the 16 picks are different logical blocks; exactly 4 of them have slots on each of 4 different indices of ctx, slot s lying on index s // 8. `block_table`: A permutation of the 32 physical slots.
All inputs are finite; a program needn't handle non-finite values.
Results may differ from a plain program's by a relative error of at most 0.0032.
Values may be sent and summed in bfloat16 or wider, within the bound.
No kernel may reach another device: no remote copies, remote signals or barrier semaphores. Data moves between devices by JAX's collectives and lax.ppermute only.
A program may use at most 64 MiB of HBM per device.

v0:
```python
import jax
import jax.numpy as jnp
import numpy as np
from jax import lax
from jax.sharding import PartitionSpec as P

BLOCK = 512
TOPK = 16


def shifted(value, axis, by):
    count = lax.axis_size(axis)
    pairs = [(i, i + by) for i in range(count) if 0 <= i + by < count]
    return lax.ppermute(value, axis, pairs)


def as_sent(value):

    def short(part):
        return part.astype(jnp.bfloat16) if part.dtype == jnp.float32 else part

    return jax.tree.map(short, value)


def partner(value, axis, bit):
    mask = 2**bit
    pairs = [(source, source ^ mask) for source in range(lax.axis_size(axis))]
    return lax.ppermute(value, axis, pairs)


def lookup(lookup_table, indices):
    entries = jnp.arange(lookup_table.shape[0], dtype=jnp.int32)
    return jnp.sum(jnp.where(indices[..., None] == entries, lookup_table, 0), axis=-1)


def owner_rank(owners):
    ordinal = jnp.arange(owners.shape[-1], dtype=jnp.int32)
    before = (owners[..., :, None] == owners[..., None, :]) & (ordinal[None, :] < ordinal[:, None])
    return jnp.sum(before, axis=-1)


def pick_rows(source, indices):
    return source[indices]


def take_blocks(blocks, indices):
    return jax.vmap(pick_rows)(blocks, indices)


def attend(query_rows, all_keys, all_values, allowed_mask):
    tile_relevance = jnp.einsum(
        "rd,kd->rk", query_rows, all_keys, preferred_element_type=jnp.float32
    )
    tile_relevance = tile_relevance * query_rows.shape[-1] ** (-0.5)
    tile_relevance = jnp.where(allowed_mask, tile_relevance, -jnp.inf)
    row_max = jnp.max(tile_relevance, axis=-1, keepdims=True)
    weights = jnp.exp(tile_relevance - row_max)
    weight_sum = jnp.sum(weights, axis=-1, keepdims=True)
    mixed = jnp.einsum(
        "rk,kd->rd", weights.astype(jnp.bfloat16), all_values, preferred_element_type=jnp.float32
    )
    return (mixed / weight_sum).astype(jnp.bfloat16)


def shards(
    queries, stretch_keys, stretch_values, cache_keys, cache_values, block_picks, block_table
):
    kv_dev, tok_dev, head_dim = stretch_keys.shape
    q_per_kv = queries.shape[0] // kv_dev
    blocks_dev = cache_keys.shape[1] // BLOCK
    ctx_size = lax.axis_size("ctx")
    ctx_index = lax.axis_index("ctx")
    per_peer = max(1, TOPK // ctx_size)
    parity = ctx_index % 2
    head_ids = lax.axis_index(("head", "tp")) * kv_dev + jnp.arange(kv_dev, dtype=jnp.int32)
    selector = head_ids[:, None] == jnp.arange(block_picks.shape[1], dtype=jnp.int32)[None, :]
    my_picks = jnp.sum(jnp.where(selector[None, :, :, None], block_picks[:, None, :, :], 0), axis=2)
    physical = lookup(block_table, my_picks)
    owners = physical // blocks_dev
    in_owner = physical % blocks_dev
    peer_rank = owner_rank(owners)
    targets = np.arange(ctx_size) * tok_dev // BLOCK
    target_owner = owners[targets]
    target_rank = peer_rank[targets]
    target_local = in_owner[targets]
    slot_ids = jnp.arange(per_peer, dtype=jnp.int32)
    matched = (target_owner[:, :, None, :] == ctx_index) & (
        target_rank[:, :, None, :] == slot_ids[None, None, :, None]
    )
    chosen = jnp.sum(jnp.where(matched, target_local[:, :, None, :], 0), axis=-1)
    usable = jnp.any(matched, axis=-1)
    chosen = jnp.transpose(chosen, (1, 0, 2)).reshape(kv_dev, ctx_size * per_peer)
    usable = jnp.transpose(usable, (1, 0, 2)).reshape(kv_dev, ctx_size * per_peer)
    my_block = ctx_index * tok_dev // BLOCK
    my_owner = lax.dynamic_index_in_dim(owners, my_block, 0, keepdims=False)
    my_rank = lax.dynamic_index_in_dim(peer_rank, my_block, 0, keepdims=False)
    my_slot = my_owner * per_peer + my_rank
    prev_keys, prev_values = shifted((stretch_keys, stretch_values), "ctx", 1)
    half_rows = BLOCK // 2
    key_halves = cache_keys.reshape(kv_dev, blocks_dev * 2, half_rows, head_dim)
    value_halves = cache_values.reshape(kv_dev, blocks_dev * 2, half_rows, head_dim)
    row_side = jnp.asarray(np.repeat(np.arange(ctx_size) % 2, per_peer), jnp.int32)
    half_index = chosen * 2 + row_side[None, :]
    sent_keys = jnp.where(usable[:, :, None, None], take_blocks(key_halves, half_index), 0).astype(
        jnp.bfloat16
    )
    sent_values = jnp.where(
        usable[:, :, None, None], take_blocks(value_halves, half_index), 0
    ).astype(jnp.bfloat16)
    got_keys, got_values = (
        lax.all_to_all(sent_keys, "ctx", split_axis=1, concat_axis=1, tiled=True),
        lax.all_to_all(sent_values, "ctx", split_axis=1, concat_axis=1, tiled=True),
    )
    mine_keys = take_blocks(got_keys, my_slot)
    mine_values = take_blocks(got_values, my_slot)
    other_keys, other_values = (
        partner(as_sent(mine_keys), "ctx", 0).astype(mine_keys.dtype),
        partner(as_sent(mine_values), "ctx", 0).astype(mine_values.dtype),
    )
    first_keys = jnp.where(parity == 0, mine_keys, other_keys)
    second_keys = jnp.where(parity == 0, other_keys, mine_keys)
    first_values = jnp.where(parity == 0, mine_values, other_values)
    second_values = jnp.where(parity == 0, other_values, mine_values)
    live_keys = jnp.concatenate([first_keys, second_keys], axis=2)
    live_values = jnp.concatenate([first_values, second_values], axis=2)
    span_cols = TOPK * BLOCK
    live_keys = live_keys.reshape(kv_dev, span_cols, head_dim)
    live_values = live_values.reshape(kv_dev, span_cols, head_dim)
    all_keys = jnp.concatenate([live_keys, prev_keys, stretch_keys], axis=1)
    all_values = jnp.concatenate([live_values, prev_values, stretch_values], axis=1)
    query_rows = queries.reshape(kv_dev, q_per_kv * tok_dev, head_dim)
    step_rows = min(512, q_per_kv * tok_dev)
    columns = jnp.arange(span_cols + 2 * tok_dev, dtype=jnp.int32)

    def one_head(packed):
        q_head, k_head, v_head = packed
        q_steps = q_head.reshape(-1, step_rows, head_dim)
        starts = jnp.arange(q_steps.shape[0], dtype=jnp.int32) * step_rows

        def one_step(packed_block_step):
            q_block, first_row = packed_block_step
            position = (first_row + jnp.arange(step_rows, dtype=jnp.int32)) % tok_dev
            cache_part = columns[None, :] < span_cols
            earlier_part = (
                (columns[None, :] >= span_cols)
                & (columns[None, :] < span_cols + tok_dev)
                & (columns[None, :] - span_cols > position[:, None])
                & (ctx_index > 0)
            )
            own_part = (columns[None, :] >= span_cols + tok_dev) & (
                columns[None, :] - span_cols - tok_dev <= position[:, None]
            )
            return attend(q_block, k_head, v_head, cache_part | earlier_part | own_part)

        return lax.map(one_step, (q_steps, starts)).reshape(q_per_kv * tok_dev, head_dim)

    result = lax.map(one_head, (query_rows, all_keys, all_values))
    return result.reshape(kv_dev * q_per_kv, tok_dev, head_dim)


def solution(mesh):
    placed = (
        P(("head", "tp"), ("groups", "ctx"), None),
        P(("head", "tp"), ("groups", "ctx"), None),
        P(("head", "tp"), ("groups", "ctx"), None),
        P(("head", "tp"), ("groups", "ctx"), None),
        P(("head", "tp"), ("groups", "ctx"), None),
        P("groups", None, None),
        P("groups"),
    )
    return jax.shard_map(
        shards,
        mesh=mesh,
        in_specs=placed,
        out_specs=P(("head", "tp"), ("groups", "ctx"), None),
        check_vma=False,
    )
```

profile of v0, /device:TPU:0, one launch (start us, length us, event | category | flops | bytes accessed | tf_op | source)
XLA Modules:
  0.0 363.8 jit_solution(13856905821156815247)
XLA Ops:
  0.0 0.1 iota_compare_fusion.3
  0.1 0.9 select_reduce_fusion.2
  1.0 0.9 select_reduce_fusion
  1.9 0.7 pad_clamp_fusion
  2.6 0.2 convert_reduce_fusion
  2.8 0.6 gather_fusion
  3.4 0.6 gather_fusion.1
  3.9 0.6 gather_fusion.2
  4.5 0.2 fusion.24
  4.7 0.2 select_reduce_fusion.1
  5.0 0.1 mul.65
  5.1 0.7 fusion.27
  5.7 0.1 reshape.259
  5.8 2.1 gather_fusion.3
  7.9 3.9 %gather_fusion.5 = bf16[32,256,128]{2,1,0:T(8,128)(2,1)} fusion(bf16[2,16,256,128]{3,2,1,0:T(8,128)(2,1)} %bitcast.67, s32[32]{0:T(128)S(1)} %reshape.259), kind=kCustom, calls=%fused_computation.5 | custom fusion | bytes 4194560 | tf_op jit(solution)/shard_map/vmap()/gather | solution.py:43
  11.8 0.1 broadcast_in_dim.137
  11.9 3.2 broadcast_select_fusion
  15.2 1.6 copy.18
  16.7 6.4 %all-to-all-start = ((bf16[2,16,256,128]{3,2,0,1:T(8,128)(2,1)}), bf16[2,16,256,128]{3,2,0,1:T(8,128)(2,1)S(1)}, u32[]{:S(2)}, u32[]{:S(2)}) async-start(bf16[2,16,256,128]{3,2,0,1:T(8,128)(2,1)} %copy.18), calls=%async_computation | async-start | bytes 4194304 | tf_op jit(solution)/shard_map/all_to_all | solution.py:111
  23.1 3.1 copy.19
  26.2 45.1 %all-to-all-done = bf16[2,16,256,128]{3,2,0,1:T(8,128)(2,1)S(1)} async-done(((bf16[2,16,256,128]{3,2,0,1:T(8,128)(2,1)}), bf16[2,16,256,128]{3,2,0,1:T(8,128)(2,1)S(1)}, u32[]{:S(2)}, u32[]{:S(2)}) %all-to-all-start) | async-done | bytes 2097184 | tf_op jit(solution)/shard_map/all_to_all | solution.py:111
  71.3 4.5 %all-to-all-start.1 = ((bf16[2,16,256,128]{3,2,0,1:T(8,128)(2,1)}), bf16[2,16,256,128]{3,2,0,1:T(8,128)(2,1)}, u32[]{:S(2)}, u32[]{:S(2)}) async-start(bf16[2,16,256,128]{3,2,0,1:T(8,128)(2,1)} %copy.19), calls=%async_computation.1 | async-start | bytes 4194304 | tf_op jit(solution)/shard_map/all_to_all | solution.py:112
  75.8 0.1 reshape.265
  75.9 2.6 gather_fusion.4
  78.5 2.0 collective-permute-start
  80.5 43.2 %all-to-all-done.1 = bf16[2,16,256,128]{3,2,0,1:T(8,128)(2,1)} async-done(((bf16[2,16,256,128]{3,2,0,1:T(8,128)(2,1)}), bf16[2,16,256,128]{3,2,0,1:T(8,128)(2,1)}, u32[]{:S(2)}, u32[]{:S(2)}) %all-to-all-start.1) | async-done | bytes 2097184 | tf_op jit(solution)/shard_map/all_to_all | solution.py:112
  123.7 3.7 %gather_fusion.6 = bf16[32,256,128]{2,1,0:T(8,128)(2,1)} fusion(bf16[2,16,256,128]{3,2,0,1:T(8,128)(2,1)} %all-to-all-done.1, s32[32]{0:T(128)S(1)} %reshape.265), kind=kCustom, calls=%fused_computation.6 | custom fusion | bytes 4194560 | tf_op jit(solution)/shard_map/vmap()/gather | solution.py:43
  127.4 3.9 %collective-permute-start.3 = (bf16[2,256,128]{2,1,0:T(8,128)(2,1)S(1)}, bf16[2,256,128]{2,1,0:T(8,128)(2,1)S(1)}, u32[]{:S(2)}, u32[]{:S(2)}) collective-permute-start(bf16[2,256,128]{2,1,0:T(8,128)(2,1)S(1)} %copy-done.5), channel_id=1, source_target_pairs={{0,4},{4,8},{8,12},{1,5},{5,9},{9,13},{2,6},{6,10},{10,14},{3,7},{... | collective-permute-start | bytes 393224 | tf_op jit(solution)/shard_map/ppermute | solution.py:14
  131.4 2.6 collective-permute-start.1
  134.0 24.2 %collective-permute-done = bf16[2,16,256,128]{3,2,1,0:T(8,128)(2,1)} collective-permute-done((bf16[2,16,256,128]{3,2,1,0:T(8,128)(2,1)S(1)}, bf16[2,16,256,128]{3,2,1,0:T(8,128)(2,1)}, u32[]{:S(2)}, u32[]{:S(2)}) %collective-permute-start) | collective-permute-done | bytes 2097184 | tf_op jit(solution)/shard_map/ppermute | solution.py:28
  158.2 43.1 %collective-permute-done.2 = bf16[2,16,256,128]{3,2,1,0:T(8,128)(2,1)} collective-permute-done((bf16[2,16,256,128]{3,2,1,0:T(8,128)(2,1)}, bf16[2,16,256,128]{3,2,1,0:T(8,128)(2,1)}, u32[]{:S(2)}, u32[]{:S(2)}) %collective-permute-start.2) | collective-permute-done | bytes 2097184 | tf_op jit(solution)/shard_map/ppermute | solution.py:28
  201.3 3.1 broadcast_select_fusion.3
  204.4 0.4 pad_maximum_fusion.3
  204.9 10.0 %pad_maximum_fusion.1 = bf16[2,8704,128]{2,1,0:T(8,128)(2,1)} fusion(bf16[2,256,128]{2,1,0:T(8,128)(2,1)S(1)} %copy-done.5, bf16[2,256,128]{2,1,0:T(8,128)(2,1)S(1)} %collective-permute-done.3, bf16[2,8192,128]{2,1,0:T(8,128)(2,1)S(1)} %bitcast.56), kind=kLoop, calls=%fused_computation.36 | loop fusion | flops 13369344 | bytes 8912896 | tf_op jit(solution)/shard_map/concatenate | solution.py:130
  214.9 0.4 pad_maximum_fusion.2
  215.3 9.9 %pad_maximum_fusion = bf16[2,8704,128]{2,1,0:T(8,128)(2,1)} fusion(bf16[2,256,128]{2,1,0:T(8,128)(2,1)S(1)} %copy-done.6, bf16[2,256,128]{2,1,0:T(8,128)(2,1)S(1)} %collective-permute-done.1, bf16[2,8192,128]{2,1,0:T(8,128)(2,1)S(1)} %bitcast.57), kind=kLoop, calls=%fused_computation.35 | loop fusion | flops 13369344 | bytes 8912896 | tf_op jit(solution)/shard_map/concatenate | solution.py:129
  225.2 136.7 %while.49 = (s32[]{:T(128)}, bf16[2,1024,128]{2,1,0:T(8,128)(2,1)S(1)}, bf16[2,1024,128]{2,1,0:T(8,128)(2,1)S(1)}, bf16[2,8704,128]{2,1,0:T(8,128)(2,1)}, bf16[2...) while((s32[]{:T(128)}, ...), condition=%wide.region_10.11_spmd.clone.clone, body=%wide.region_5.10_spmd.clone.clone.sunk | while | flops 2344288768 | bytes 68473648 | solution.py:157
  225.2 3.9 %dynamic-slice_bitcast_fusion.3 = (bf16[8704,128]{1,0:T(8,128)(2,1)}, bf16[8704,128]{1,0:T(8,128)(2,1)}) fusion(bf16[2,8704,128]{2,1,0:T(8,128)(2,1)} %get-tuple-element.681, s32[]{:T(128)} %get-tuple-element.668, bf16[2,8704,128]{2,1,0:T(8,128)(2,1)} %get-tuple-element.680), kind=kLoop, calls=%fused_computation.30.clone.1 | loop fusion | bytes 8912900 | tf_op jit(solution)/shard_map/while/body/jit(dynamic_index_in_dim)/squeeze | solution.py:157
  229.2 64.4 %while.50 = (s32[]{:T(128)}, bf16[2,512,128]{2,1,0:T(8,128)(2,1)S(1)}, s32[8704]{0:T(1024)S(1)}, s32[2]{0:T(128)S(1)}, pred[]{:T(512)}, /*index=5*/bf16[2,512,12...) while((s32[]{:T(128)}, ...), condition=%wide.region_9.9_spmd.clone, body=%wide.region_6.8_spmd.clone.sunk | while | flops 2344288768 | bytes 58477172 | solution.py:155
  229.2 0.6 dynamic_slice.85
  229.8 0.6 add_select_fusion.2
  230.4 13.1 %fusion.43 = (f32[512]{0:T(512)S(1)}, f32[512,8704]{1,0:T(8,128)}) fusion(bf16[8704,128]{1,0:T(8,128)(2,1)} %get-tuple-element.656, bf16[2,512,128]{2,1,0:T(8,128)(2,1)S(1)} %get-tuple-element.655, s32[]{:T(128)} %get-tuple-element.641, s32[8704]{0:T(1024)S(1)} %get-tuple-element.625, pred[8704]{0:T(1024)(128)(4,1)S(1)} %get-tuple-element.626, ...), kind=kOutput, calls=%fused_computation.75.clone.1 | convolution fusion | flops 1185414656 | bytes 20290564 | tf_op jit(solution)/shard_map/while/body/eval_jaxpr/while/body/eval_jaxpr/rd,kd->rk/dot_general | solution.py:51
  243.5 8.5 %fusion.44 = f32[512]{0:T(512)S(1)} fusion(f32[512,8704]{1,0:T(8,128)} %get-tuple-element.630, f32[512]{0:T(512)S(1)} %get-tuple-element.631), kind=kLoop, calls=%fused_computation.10.clone.1 | loop fusion | flops 8912384 | bytes 17829888 | tf_op jit(solution)/shard_map/while/body/eval_jaxpr/while/body/eval_jaxpr/reduce_sum | solution.py:58
  252.1 9.3 %fusion.45 = bf16[2,512,128]{2,1,0:T(8,128)(2,1)S(1)} fusion(bf16[2,512,128]{2,1,0:T(8,128)(2,1)S(1)} %get-tuple-element.642, s32[]{:T(128)} %get-tuple-element.641, bf16[8704,128]{1,0:T(8,128)(2,1)} %get-tuple-element.657, f32[512,8704]{1,0:T(8,128)} %get-tuple-element.630, f32[512]{0:T(512)S(1)} %get-tuple-element.631, f32[512]{0:T(512)S(1)} %fusion.44), kind=kOutput, calls=%fused_computation.17.clone.1 | convolution fusion | flops 1149894656 | bytes 20189188 | tf_op jit(solution)/shard_map/while/body/eval_jaxpr/while/body/eval_jaxpr/rk,kd->rd/dot_general | solution.py:59
  261.4 0.6 dynamic_slice.85
  262.0 0.6 add_select_fusion.2
  262.6 13.1 %fusion.43 = (f32[512]{0:T(512)S(1)}, f32[512,8704]{1,0:T(8,128)}) fusion(bf16[8704,128]{1,0:T(8,128)(2,1)} %get-tuple-element.656, bf16[2,512,128]{2,1,0:T(8,128)(2,1)S(1)} %get-tuple-element.655, s32[]{:T(128)} %get-tuple-element.641, s32[8704]{0:T(1024)S(1)} %get-tuple-element.625, pred[8704]{0:T(1024)(128)(4,1)S(1)} %get-tuple-element.626, ...), kind=kOutput, calls=%fused_computation.75.clone.1 | convolution fusion | flops 1185414656 | bytes 20290564 | tf_op jit(solution)/shard_map/while/body/eval_jaxpr/while/body/eval_jaxpr/rd,kd->rk/dot_general | solution.py:51
  275.7 8.5 %fusion.44 = f32[512]{0:T(512)S(1)} fusion(f32[512,8704]{1,0:T(8,128)} %get-tuple-element.630, f32[512]{0:T(512)S(1)} %get-tuple-element.631), kind=kLoop, calls=%fused_computation.10.clone.1 | loop fusion | flops 8912384 | bytes 17829888 | tf_op jit(solution)/shard_map/while/body/eval_jaxpr/while/body/eval_jaxpr/reduce_sum | solution.py:58
  284.2 9.3 %fusion.45 = bf16[2,512,128]{2,1,0:T(8,128)(2,1)S(1)} fusion(bf16[2,512,128]{2,1,0:T(8,128)(2,1)S(1)} %get-tuple-element.642, s32[]{:T(128)} %get-tuple-element.641, bf16[8704,128]{1,0:T(8,128)(2,1)} %get-tuple-element.657, f32[512,8704]{1,0:T(8,128)} %get-tuple-element.630, f32[512]{0:T(512)S(1)} %get-tuple-element.631, f32[512]{0:T(512)S(1)} %fusion.44), kind=kOutput, calls=%fused_computation.17.clone.1 | convolution fusion | flops 1149894656 | bytes 20189188 | tf_op jit(solution)/shard_map/while/body/eval_jaxpr/while/body/eval_jaxpr/rk,kd->rd/dot_general | solution.py:59
  293.6 3.9 %dynamic-slice_bitcast_fusion.3 = (bf16[8704,128]{1,0:T(8,128)(2,1)}, bf16[8704,128]{1,0:T(8,128)(2,1)}) fusion(bf16[2,8704,128]{2,1,0:T(8,128)(2,1)} %get-tuple-element.681, s32[]{:T(128)} %get-tuple-element.668, bf16[2,8704,128]{2,1,0:T(8,128)(2,1)} %get-tuple-element.680), kind=kLoop, calls=%fused_computation.30.clone.1 | loop fusion | bytes 8912900 | tf_op jit(solution)/shard_map/while/body/jit(dynamic_index_in_dim)/squeeze | solution.py:157
  297.5 64.4 %while.50 = (s32[]{:T(128)}, bf16[2,512,128]{2,1,0:T(8,128)(2,1)S(1)}, s32[8704]{0:T(1024)S(1)}, s32[2]{0:T(128)S(1)}, pred[]{:T(512)}, /*index=5*/bf16[2,512,12...) while((s32[]{:T(128)}, ...), condition=%wide.region_9.9_spmd.clone, body=%wide.region_6.8_spmd.clone.sunk | while | flops 2344288768 | bytes 58477172 | solution.py:155
  297.6 0.6 dynamic_slice.85
  298.2 0.6 add_select_fusion.2
  298.8 13.1 %fusion.43 = (f32[512]{0:T(512)S(1)}, f32[512,8704]{1,0:T(8,128)}) fusion(bf16[8704,128]{1,0:T(8,128)(2,1)} %get-tuple-element.656, bf16[2,512,128]{2,1,0:T(8,128)(2,1)S(1)} %get-tuple-element.655, s32[]{:T(128)} %get-tuple-element.641, s32[8704]{0:T(1024)S(1)} %get-tuple-element.625, pred[8704]{0:T(1024)(128)(4,1)S(1)} %get-tuple-element.626, ...), kind=kOutput, calls=%fused_computation.75.clone.1 | convolution fusion | flops 1185414656 | bytes 20290564 | tf_op jit(solution)/shard_map/while/body/eval_jaxpr/while/body/eval_jaxpr/rd,kd->rk/dot_general | solution.py:51
  311.9 8.5 %fusion.44 = f32[512]{0:T(512)S(1)} fusion(f32[512,8704]{1,0:T(8,128)} %get-tuple-element.630, f32[512]{0:T(512)S(1)} %get-tuple-element.631), kind=kLoop, calls=%fused_computation.10.clone.1 | loop fusion | flops 8912384 | bytes 17829888 | tf_op jit(solution)/shard_map/while/body/eval_jaxpr/while/body/eval_jaxpr/reduce_sum | solution.py:58
  320.4 9.3 %fusion.45 = bf16[2,512,128]{2,1,0:T(8,128)(2,1)S(1)} fusion(bf16[2,512,128]{2,1,0:T(8,128)(2,1)S(1)} %get-tuple-element.642, s32[]{:T(128)} %get-tuple-element.641, bf16[8704,128]{1,0:T(8,128)(2,1)} %get-tuple-element.657, f32[512,8704]{1,0:T(8,128)} %get-tuple-element.630, f32[512]{0:T(512)S(1)} %get-tuple-element.631, f32[512]{0:T(512)S(1)} %fusion.44), kind=kOutput, calls=%fused_computation.17.clone.1 | convolution fusion | flops 1149894656 | bytes 20189188 | tf_op jit(solution)/shard_map/while/body/eval_jaxpr/while/body/eval_jaxpr/rk,kd->rd/dot_general | solution.py:59
  329.8 0.6 dynamic_slice.85
  330.4 0.6 add_select_fusion.2
  331.0 13.1 %fusion.43 = (f32[512]{0:T(512)S(1)}, f32[512,8704]{1,0:T(8,128)}) fusion(bf16[8704,128]{1,0:T(8,128)(2,1)} %get-tuple-element.656, bf16[2,512,128]{2,1,0:T(8,128)(2,1)S(1)} %get-tuple-element.655, s32[]{:T(128)} %get-tuple-element.641, s32[8704]{0:T(1024)S(1)} %get-tuple-element.625, pred[8704]{0:T(1024)(128)(4,1)S(1)} %get-tuple-element.626, ...), kind=kOutput, calls=%fused_computation.75.clone.1 | convolution fusion | flops 1185414656 | bytes 20290564 | tf_op jit(solution)/shard_map/while/body/eval_jaxpr/while/body/eval_jaxpr/rd,kd->rk/dot_general | solution.py:51
  344.1 8.5 %fusion.44 = f32[512]{0:T(512)S(1)} fusion(f32[512,8704]{1,0:T(8,128)} %get-tuple-element.630, f32[512]{0:T(512)S(1)} %get-tuple-element.631), kind=kLoop, calls=%fused_computation.10.clone.1 | loop fusion | flops 8912384 | bytes 17829888 | tf_op jit(solution)/shard_map/while/body/eval_jaxpr/while/body/eval_jaxpr/reduce_sum | solution.py:58
  352.6 9.3 %fusion.45 = bf16[2,512,128]{2,1,0:T(8,128)(2,1)S(1)} fusion(bf16[2,512,128]{2,1,0:T(8,128)(2,1)S(1)} %get-tuple-element.642, s32[]{:T(128)} %get-tuple-element.641, bf16[8704,128]{1,0:T(8,128)(2,1)} %get-tuple-element.657, f32[512,8704]{1,0:T(8,128)} %get-tuple-element.630, f32[512]{0:T(512)S(1)} %get-tuple-element.631, f32[512]{0:T(512)S(1)} %fusion.44), kind=kOutput, calls=%fused_computation.17.clone.1 | convolution fusion | flops 1149894656 | bytes 20189188 | tf_op jit(solution)/shard_map/while/body/eval_jaxpr/while/body/eval_jaxpr/rk,kd->rd/dot_general | solution.py:59
  362.0 0.0 copy-start.7
  362.0 0.8 copy-done.7
  362.8 1.0 copy-done.1
  (43 shorter events, 0.4 us)
Async XLA Ops:
  0.0 5.8 %copy-start = (bf16[2,4096,128]{2,1,0:T(8,128)(2,1)S(1)}, bf16[2,4096,128]{2,1,0:T(8,128)(2,1)}, u32[]{:S(2)}) copy-start(bf16[2,4096,128]{2,1,0:T(8,128)(2,1)} %param.19) | copy-start | bytes 6291460
  7.9 4.0 %copy-start.3 = (bf16[32,256,128]{2,1,0:T(8,128)(2,1)S(1)}, bf16[32,256,128]{2,1,0:T(8,128)(2,1)}, u32[]{:S(2)}) copy-start(bf16[32,256,128]{2,1,0:T(8,128)(2,1)} %gather_fusion.3) | copy-start | bytes 6291460
  16.7 54.6 %all-to-all-start = ((bf16[2,16,256,128]{3,2,0,1:T(8,128)(2,1)}), bf16[2,16,256,128]{3,2,0,1:T(8,128)(2,1)S(1)}, u32[]{:S(2)}, u32[]{:S(2)}) async-start(bf16[2,16,256,128]{3,2,0,1:T(8,128)(2,1)} %copy.18), calls=%async_computation | async-start | bytes 4194304 | tf_op jit(solution)/shard_map/all_to_all | solution.py:111
  71.3 4.5 %copy-start.2 = (bf16[2,16,256,128]{3,2,0,1:T(8,128)(2,1)}, bf16[2,16,256,128]{3,2,0,1:T(8,128)(2,1)S(1)}, u32[]{:S(2)}) copy-start(bf16[2,16,256,128]{3,2,0,1:T(8,128)(2,1)S(1)} %all-to-all-done) | copy-start | bytes 6291460
  71.3 52.4 %all-to-all-start.1 = ((bf16[2,16,256,128]{3,2,0,1:T(8,128)(2,1)}), bf16[2,16,256,128]{3,2,0,1:T(8,128)(2,1)}, u32[]{:S(2)}, u32[]{:S(2)}) async-start(bf16[2,16,256,128]{3,2,0,1:T(8,128)(2,1)} %copy.19), calls=%async_computation.1 | async-start | bytes 4194304 | tf_op jit(solution)/shard_map/all_to_all | solution.py:112
  75.9 51.5 %copy-start.5 = (bf16[2,256,128]{2,1,0:T(8,128)(2,1)S(1)}, bf16[2,256,128]{2,1,0:T(8,128)(2,1)}, u32[]{:S(2)}) copy-start(bf16[2,256,128]{2,1,0:T(8,128)(2,1)} %param.18) | copy-start | bytes 393220
  75.9 55.5 %copy-start.6 = (bf16[2,256,128]{2,1,0:T(8,128)(2,1)S(1)}, bf16[2,256,128]{2,1,0:T(8,128)(2,1)}, u32[]{:S(2)}) copy-start(bf16[2,256,128]{2,1,0:T(8,128)(2,1)} %param.17) | copy-start | bytes 393220
  78.5 79.7 %collective-permute-start = (bf16[2,16,256,128]{3,2,1,0:T(8,128)(2,1)S(1)}, bf16[2,16,256,128]{3,2,1,0:T(8,128)(2,1)}, u32[]{:S(2)}, u32[]{:S(2)}) collective-permute-start(bf16[2,16,256,128]{3,2,1,0:T(8,128)(2,1)S(1)} %bitcast.58), channel_id=1, source_target_pairs={{0,4},{4,0},{8,12},{12,8},{1,5},{5,1},{9,13},{13,9},{2,6},{6,2},{1... | collective-permute-start | bytes 6291464 | tf_op jit(solution)/shard_map/ppermute | solution.py:28
  127.4 73.9 %collective-permute-start.2 = (bf16[2,16,256,128]{3,2,1,0:T(8,128)(2,1)}, bf16[2,16,256,128]{3,2,1,0:T(8,128)(2,1)}, u32[]{:S(2)}, u32[]{:S(2)}) collective-permute-start(bf16[2,16,256,128]{3,2,1,0:T(8,128)(2,1)} %bitcast.60), channel_id=1, source_target_pairs={{0,4},{4,0},{8,12},{12,8},{1,5},{5,1},{9,13},{13,9},{2,6},{6,2},{1... | collective-permute-start | bytes 6291464 | tf_op jit(solution)/shard_map/ppermute | solution.py:28
  127.4 77.5 %collective-permute-start.3 = (bf16[2,256,128]{2,1,0:T(8,128)(2,1)S(1)}, bf16[2,256,128]{2,1,0:T(8,128)(2,1)S(1)}, u32[]{:S(2)}, u32[]{:S(2)}) collective-permute-start(bf16[2,256,128]{2,1,0:T(8,128)(2,1)S(1)} %copy-done.5), channel_id=1, source_target_pairs={{0,4},{4,8},{8,12},{1,5},{5,9},{9,13},{2,6},{6,10},{10,14},{3,7},{... | collective-permute-start | bytes 393224 | tf_op jit(solution)/shard_map/ppermute | solution.py:14
  131.4 83.9 %collective-permute-start.1 = (bf16[2,256,128]{2,1,0:T(8,128)(2,1)S(1)}, bf16[2,256,128]{2,1,0:T(8,128)(2,1)S(1)}, u32[]{:S(2)}, u32[]{:S(2)}) collective-permute-start(bf16[2,256,128]{2,1,0:T(8,128)(2,1)S(1)} %copy-done.6), channel_id=1, source_target_pairs={{0,4},{4,8},{8,12},{1,5},{5,9},{9,13},{2,6},{6,10},{10,14},{3,7},{... | collective-permute-start | bytes 393224 | tf_op jit(solution)/shard_map/ppermute | solution.py:14
  215.3 9.9 %copy-start.4 = (bf16[8,256,128]{2,1,0:T(8,128)(2,1)S(1)}, bf16[8,256,128]{2,1,0:T(8,128)(2,1)}, u32[]{:S(2)}) copy-start(bf16[8,256,128]{2,1,0:T(8,128)(2,1)} %param.16) | copy-start | bytes 1572868
  362.0 0.8 copy-start.7
  362.0 1.8 copy-start.1
where the time goes:
time: 365 us; the launch traced here: 364 us
  waiting for transfers between devices  156 us (43%)
  matrix products  89.4 us (24%)
  other arithmetic  67.8 us (19%)
  local copies, waits for them, and re-layouts  31.2 us (9%)
  starting transfers between devices  19.4 us (5%)
    ppermute x2, waiting for transfers between devices, partner(): return lax.ppermute(value, axis, pairs)  67.3 us
    dot_general x4, matrix products, attend(): jnp.einsum('rd,kd->rk', query_rows, all_keys, preferred_element_type=jnp....  52.3 us
    all_to_all x1, waiting for transfers between devices, shards(): lax.all_to_all(sent_keys, 'ctx', split_axis=1, concat_axis=1, tiled=True)  45.1 us
    all_to_all x1, waiting for transfers between devices, shards(): lax.all_to_all(sent_values, 'ctx', split_axis=1, concat_axis=1, tiled=True)  43.2 us
    dot_general x4, matrix products, attend(): jnp.einsum('rk,kd->rd', weights.astype(jnp.bfloat16), all_values, preferr...  37.1 us
    reduce_sum x4, other arithmetic, attend(): weight_sum = jnp.sum(weights, axis=-1, keepdims=True)  34.2 us
    gather x6, local copies, waits for them, and re-layouts, pick_rows(): return source[indices]  12.5 us
    concatenate x1, other arithmetic, shards(): jnp.concatenate([live_values, prev_values, stretch_values], axis=1)  9.97 us
  transfers between devices with their start and end apart: 6, of which 4 were waited for; matrix products, arithmetic and copies ran while one was open for 6% of the time, Pallas kernels for 0%

commit v1 on v0

--- a/solution.py
+++ b/solution.py
@@ -108,7 +108,12 @@
         usable[:, :, None, None], take_blocks(value_halves, half_index), 0
     ).astype(jnp.bfloat16)
     got_keys, got_values = (
-        lax.all_to_all(sent_keys, "ctx", split_axis=1, concat_axis=1, tiled=True),
+        jnp.concatenate(
+            lax.all_to_all(
+                jnp.stack(jnp.split(sent_keys, lax.axis_size("ctx"), axis=1)), "ctx", 0, 0
+            ),
+            axis=1,
+        ),
         lax.all_to_all(sent_values, "ctx", split_axis=1, concat_axis=1, tiled=True),
     )
     mine_keys = take_blocks(got_keys, my_slot)

time: 365 us -> 365 us (level)
  transfers between devices with their start and end apart: 6 -> 6, of which waited for: 4 -> 4; matrix products, arithmetic and copies ran while one was open for 6% -> 7% of each run, Pallas kernels for 0% -> 0%
where the time goes in v1:
time: 365 us; the launch traced here: 364 us
  waiting for transfers between devices  154 us (42%)
  matrix products  89.4 us (24%)
  other arithmetic  70 us (19%)
  local copies, waits for them, and re-layouts  31.2 us (9%)
  starting transfers between devices  19.4 us (5%)
    ppermute x2, waiting for transfers between devices, partner(): return lax.ppermute(value, axis, pairs)  67.3 us
    dot_general x4, matrix products, attend(): jnp.einsum('rd,kd->rk', query_rows, all_keys, preferred_element_type=jnp....  52.3 us
    all_to_all x1, waiting for transfers between devices, shards(): lax.all_to_all(jnp.stack(jnp.split(sent_keys, lax.axis_size('ctx'), axis=...  45 us
    all_to_all x1, waiting for transfers between devices, shards(): lax.all_to_all(sent_values, 'ctx', split_axis=1, concat_axis=1, tiled=True)  41.7 us
    dot_general x4, matrix products, attend(): jnp.einsum('rk,kd->rd', weights.astype(jnp.bfloat16), all_values, preferr...  37.1 us
    reduce_sum x4, other arithmetic, attend(): weight_sum = jnp.sum(weights, axis=-1, keepdims=True)  34.2 us
    gather x6, local copies, waits for them, and re-layouts, pick_rows(): return source[indices]  12.3 us
    concatenate x1, other arithmetic, shards(): jnp.concatenate([live_values, prev_values, stretch_values], axis=1)  9.97 us
  transfers between devices with their start and end apart: 6, of which 4 were waited for; matrix products, arithmetic and copies ran while one was open for 7% of the time, Pallas kernels for 0%

profile of v1, /device:TPU:0, one launch (start us, length us, event | category | flops | bytes accessed | tf_op | source)
XLA Modules:
  0.0 364.5 jit_solution(1419883446588091762)
XLA Ops:
  0.1 0.9 select_reduce_fusion.2
  1.0 0.9 select_reduce_fusion
  1.9 0.7 pad_clamp_fusion
  2.6 0.6 gather_fusion
  3.1 0.2 convert_reduce_fusion
  3.4 0.6 gather_fusion.1
  3.9 0.6 gather_fusion.2
  4.5 0.2 fusion.24
  4.7 0.2 select_reduce_fusion.1
  5.0 0.1 mul.65
  5.1 0.7 fusion.27
  5.7 0.1 reshape.267
  5.8 2.1 gather_fusion.5
  8.0 3.7 %gather_fusion.3 = bf16[32,256,128]{2,1,0:T(8,128)(2,1)} fusion(bf16[2,16,256,128]{3,2,1,0:T(8,128)(2,1)} %bitcast.79, s32[32]{0:T(128)S(1)} %reshape.267), kind=kCustom, calls=%fused_computation.3 | custom fusion | bytes 4194560 | tf_op jit(solution)/shard_map/vmap()/gather | solution.py:43
  11.7 0.1 broadcast_in_dim.137
  11.8 3.9 %broadcast_select_fusion = (bf16[2,16,256,128]{3,2,1,0:T(8,128)(2,1)}, bf16[2,16,256,128]{3,2,1,0:T(8,128)(2,1)S(1)}) fusion(bf16[2,16,256,128]{3,2,1,0:T(8,128)(2,1)} %bitcast.74, pred[2,16]{1,0:T(4,128)(4,1)S(1)} %broadcast_in_dim.137, bf16[2,16,256,128]{3,2,1,0:T(8,128)(2,1)} %bitcast.75), kind=kLoop, calls=%fused_computation.40 | loop fusion | flops 2097152 | bytes 8388640 | tf_op jit(solution)/shard_map/jit(_where)/select_n | solution.py:107
  15.7 0.1 slice_bitcast_fusion.3
  15.8 1.6 pad_maximum_fusion.4
  17.4 6.4 %all-to-all-start = ((bf16[4,2,4,256,128]{4,3,2,1,0:T(8,128)(2,1)}), bf16[4,2,4,256,128]{4,3,2,1,0:T(8,128)(2,1)S(1)}, u32[]{:S(2)}, u32[]{:S(2)}) async-start(bf16[4,2,4,256,128]{4,3,2,1,0:T(8,128)(2,1)} %pad_maximum_fusion.4), calls=%async_computation | async-start | bytes 4194304 | tf_op jit(solution)/shard_map/all_to_all | solution.py:112
  23.7 3.1 copy.21
  26.9 45.0 %all-to-all-done = bf16[4,2,4,256,128]{4,3,2,1,0:T(8,128)(2,1)S(1)} async-done(((bf16[4,2,4,256,128]{4,3,2,1,0:T(8,128)(2,1)}), bf16[4,2,4,256,128]{4,3,2,1,0:T(8,128)(2,1)S(1)}, u32[]{:S(2)}, u32[]{:S(2)}) %all-to-all-start) | async-done | bytes 2097184 | tf_op jit(solution)/shard_map/all_to_all | solution.py:112
  71.9 4.4 %all-to-all-start.1 = ((bf16[2,16,256,128]{3,2,0,1:T(8,128)(2,1)}), bf16[2,16,256,128]{3,2,0,1:T(8,128)(2,1)}, u32[]{:S(2)}, u32[]{:S(2)}) async-start(bf16[2,16,256,128]{3,2,0,1:T(8,128)(2,1)} %copy.21), calls=%async_computation.1 | async-start | bytes 4194304 | tf_op jit(solution)/shard_map/all_to_all | solution.py:117
  76.4 0.1 reshape.273
  76.5 1.5 copy.20
  78.0 2.5 gather_fusion.4
  80.6 2.0 collective-permute-start
  82.6 41.7 %all-to-all-done.1 = bf16[2,16,256,128]{3,2,0,1:T(8,128)(2,1)} async-done(((bf16[2,16,256,128]{3,2,0,1:T(8,128)(2,1)}), bf16[2,16,256,128]{3,2,0,1:T(8,128)(2,1)}, u32[]{:S(2)}, u32[]{:S(2)}) %all-to-all-start.1) | async-done | bytes 2097184 | tf_op jit(solution)/shard_map/all_to_all | solution.py:117
  124.3 3.7 %gather_fusion.6 = bf16[32,256,128]{2,1,0:T(8,128)(2,1)} fusion(bf16[2,16,256,128]{3,2,0,1:T(8,128)(2,1)} %all-to-all-done.1, s32[32]{0:T(128)S(1)} %reshape.273), kind=kCustom, calls=%fused_computation.6 | custom fusion | bytes 4194560 | tf_op jit(solution)/shard_map/vmap()/gather | solution.py:43
  128.1 3.9 %collective-permute-start.3 = (bf16[2,256,128]{2,1,0:T(8,128)(2,1)S(1)}, bf16[2,256,128]{2,1,0:T(8,128)(2,1)S(1)}, u32[]{:S(2)}, u32[]{:S(2)}) collective-permute-start(bf16[2,256,128]{2,1,0:T(8,128)(2,1)S(1)} %copy-done.3), channel_id=1, source_target_pairs={{0,4},{4,8},{8,12},{1,5},{5,9},{9,13},{2,6},{6,10},{10,14},{3,7},{... | collective-permute-start | bytes 393224 | tf_op jit(solution)/shard_map/ppermute | solution.py:14
  132.0 2.6 collective-permute-start.1
  134.7 24.2 %collective-permute-done = bf16[2,16,256,128]{3,2,1,0:T(8,128)(2,1)} collective-permute-done((bf16[2,16,256,128]{3,2,1,0:T(8,128)(2,1)S(1)}, bf16[2,16,256,128]{3,2,1,0:T(8,128)(2,1)}, u32[]{:S(2)}, u32[]{:S(2)}) %collective-permute-start) | collective-permute-done | bytes 2097184 | tf_op jit(solution)/shard_map/ppermute | solution.py:28
  158.8 43.1 %collective-permute-done.2 = bf16[2,16,256,128]{3,2,1,0:T(8,128)(2,1)} collective-permute-done((bf16[2,16,256,128]{3,2,1,0:T(8,128)(2,1)}, bf16[2,16,256,128]{3,2,1,0:T(8,128)(2,1)}, u32[]{:S(2)}, u32[]{:S(2)}) %collective-permute-start.2) | collective-permute-done | bytes 2097184 | tf_op jit(solution)/shard_map/ppermute | solution.py:28
  202.0 3.1 broadcast_select_fusion.3
  205.1 0.4 pad_maximum_fusion.3
  205.5 10.0 %pad_maximum_fusion.1 = bf16[2,8704,128]{2,1,0:T(8,128)(2,1)} fusion(bf16[2,256,128]{2,1,0:T(8,128)(2,1)S(1)} %copy-done.3, bf16[2,256,128]{2,1,0:T(8,128)(2,1)S(1)} %collective-permute-done.3, bf16[2,8192,128]{2,1,0:T(8,128)(2,1)S(1)} %bitcast.67), kind=kLoop, calls=%fused_computation.36 | loop fusion | flops 13369344 | bytes 8912896 | tf_op jit(solution)/shard_map/concatenate | solution.py:135
  215.5 0.4 pad_maximum_fusion.2
  216.0 9.9 %pad_maximum_fusion = bf16[2,8704,128]{2,1,0:T(8,128)(2,1)} fusion(bf16[2,256,128]{2,1,0:T(8,128)(2,1)S(1)} %copy-done.4, bf16[2,256,128]{2,1,0:T(8,128)(2,1)S(1)} %collective-permute-done.1, bf16[2,8192,128]{2,1,0:T(8,128)(2,1)S(1)} %bitcast.68), kind=kLoop, calls=%fused_computation.35 | loop fusion | flops 13369344 | bytes 8912896 | tf_op jit(solution)/shard_map/concatenate | solution.py:134
  225.8 136.8 %while.49 = (s32[]{:T(128)}, bf16[2,1024,128]{2,1,0:T(8,128)(2,1)S(1)}, bf16[2,1024,128]{2,1,0:T(8,128)(2,1)S(1)}, bf16[2,8704,128]{2,1,0:T(8,128)(2,1)}, bf16[2...) while((s32[]{:T(128)}, ...), condition=%wide.region_10.11_spmd.clone.clone, body=%wide.region_5.10_spmd.clone.clone.sunk | while | flops 2344288768 | bytes 68473648 | solution.py:162
  225.8 3.9 %dynamic-slice_bitcast_fusion.3 = (bf16[8704,128]{1,0:T(8,128)(2,1)}, bf16[8704,128]{1,0:T(8,128)(2,1)}) fusion(bf16[2,8704,128]{2,1,0:T(8,128)(2,1)} %get-tuple-element.685, s32[]{:T(128)} %get-tuple-element.672, bf16[2,8704,128]{2,1,0:T(8,128)(2,1)} %get-tuple-element.684), kind=kLoop, calls=%fused_computation.30.clone.1 | loop fusion | bytes 8912900 | tf_op jit(solution)/shard_map/while/body/jit(dynamic_index_in_dim)/squeeze | solution.py:162
  229.8 64.4 %while.50 = (s32[]{:T(128)}, bf16[2,512,128]{2,1,0:T(8,128)(2,1)S(1)}, s32[8704]{0:T(1024)S(1)}, s32[2]{0:T(128)S(1)}, pred[]{:T(512)}, /*index=5*/bf16[2,512,12...) while((s32[]{:T(128)}, ...), condition=%wide.region_9.9_spmd.clone, body=%wide.region_6.8_spmd.clone.sunk | while | flops 2344288768 | bytes 58477172 | solution.py:160
  229.8 0.6 dynamic_slice.85
  230.5 0.6 add_select_fusion.2
  231.1 13.1 %fusion.43 = (f32[512]{0:T(512)S(1)}, f32[512,8704]{1,0:T(8,128)}) fusion(bf16[8704,128]{1,0:T(8,128)(2,1)} %get-tuple-element.660, bf16[2,512,128]{2,1,0:T(8,128)(2,1)S(1)} %get-tuple-element.659, s32[]{:T(128)} %get-tuple-element.645, s32[8704]{0:T(1024)S(1)} %get-tuple-element.629, pred[8704]{0:T(1024)(128)(4,1)S(1)} %get-tuple-element.630, ...), kind=kOutput, calls=%fused_computation.80.clone.1 | convolution fusion | flops 1185414656 | bytes 20290564 | tf_op jit(solution)/shard_map/while/body/eval_jaxpr/while/body/eval_jaxpr/rd,kd->rk/dot_general | solution.py:51
  244.2 8.5 %fusion.44 = f32[512]{0:T(512)S(1)} fusion(f32[512,8704]{1,0:T(8,128)} %get-tuple-element.634, f32[512]{0:T(512)S(1)} %get-tuple-element.635), kind=kLoop, calls=%fused_computation.10.clone.1 | loop fusion | flops 8912384 | bytes 17829888 | tf_op jit(solution)/shard_map/while/body/eval_jaxpr/while/body/eval_jaxpr/reduce_sum | solution.py:58
  252.7 9.3 %fusion.45 = bf16[2,512,128]{2,1,0:T(8,128)(2,1)S(1)} fusion(bf16[2,512,128]{2,1,0:T(8,128)(2,1)S(1)} %get-tuple-element.646, s32[]{:T(128)} %get-tuple-element.645, bf16[8704,128]{1,0:T(8,128)(2,1)} %get-tuple-element.661, f32[512,8704]{1,0:T(8,128)} %get-tuple-element.634, f32[512]{0:T(512)S(1)} %get-tuple-element.635, f32[512]{0:T(512)S(1)} %fusion.44), kind=kOutput, calls=%fused_computation.17.clone.1 | convolution fusion | flops 1149894656 | bytes 20189188 | tf_op jit(solution)/shard_map/while/body/eval_jaxpr/while/body/eval_jaxpr/rk,kd->rd/dot_general | solution.py:59
  262.0 0.6 dynamic_slice.85
  262.7 0.6 add_select_fusion.2
  263.3 13.1 %fusion.43 = (f32[512]{0:T(512)S(1)}, f32[512,8704]{1,0:T(8,128)}) fusion(bf16[8704,128]{1,0:T(8,128)(2,1)} %get-tuple-element.660, bf16[2,512,128]{2,1,0:T(8,128)(2,1)S(1)} %get-tuple-element.659, s32[]{:T(128)} %get-tuple-element.645, s32[8704]{0:T(1024)S(1)} %get-tuple-element.629, pred[8704]{0:T(1024)(128)(4,1)S(1)} %get-tuple-element.630, ...), kind=kOutput, calls=%fused_computation.80.clone.1 | convolution fusion | flops 1185414656 | bytes 20290564 | tf_op jit(solution)/shard_map/while/body/eval_jaxpr/while/body/eval_jaxpr/rd,kd->rk/dot_general | solution.py:51
  276.4 8.5 %fusion.44 = f32[512]{0:T(512)S(1)} fusion(f32[512,8704]{1,0:T(8,128)} %get-tuple-element.634, f32[512]{0:T(512)S(1)} %get-tuple-element.635), kind=kLoop, calls=%fused_computation.10.clone.1 | loop fusion | flops 8912384 | bytes 17829888 | tf_op jit(solution)/shard_map/while/body/eval_jaxpr/while/body/eval_jaxpr/reduce_sum | solution.py:58
  284.9 9.3 %fusion.45 = bf16[2,512,128]{2,1,0:T(8,128)(2,1)S(1)} fusion(bf16[2,512,128]{2,1,0:T(8,128)(2,1)S(1)} %get-tuple-element.646, s32[]{:T(128)} %get-tuple-element.645, bf16[8704,128]{1,0:T(8,128)(2,1)} %get-tuple-element.661, f32[512,8704]{1,0:T(8,128)} %get-tuple-element.634, f32[512]{0:T(512)S(1)} %get-tuple-element.635, f32[512]{0:T(512)S(1)} %fusion.44), kind=kOutput, calls=%fused_computation.17.clone.1 | convolution fusion | flops 1149894656 | bytes 20189188 | tf_op jit(solution)/shard_map/while/body/eval_jaxpr/while/body/eval_jaxpr/rk,kd->rd/dot_general | solution.py:59
  294.3 3.9 %dynamic-slice_bitcast_fusion.3 = (bf16[8704,128]{1,0:T(8,128)(2,1)}, bf16[8704,128]{1,0:T(8,128)(2,1)}) fusion(bf16[2,8704,128]{2,1,0:T(8,128)(2,1)} %get-tuple-element.685, s32[]{:T(128)} %get-tuple-element.672, bf16[2,8704,128]{2,1,0:T(8,128)(2,1)} %get-tuple-element.684), kind=kLoop, calls=%fused_computation.30.clone.1 | loop fusion | bytes 8912900 | tf_op jit(solution)/shard_map/while/body/jit(dynamic_index_in_dim)/squeeze | solution.py:162
  298.2 64.4 %while.50 = (s32[]{:T(128)}, bf16[2,512,128]{2,1,0:T(8,128)(2,1)S(1)}, s32[8704]{0:T(1024)S(1)}, s32[2]{0:T(128)S(1)}, pred[]{:T(512)}, /*index=5*/bf16[2,512,12...) while((s32[]{:T(128)}, ...), condition=%wide.region_9.9_spmd.clone, body=%wide.region_6.8_spmd.clone.sunk | while | flops 2344288768 | bytes 58477172 | solution.py:160
  298.3 0.6 dynamic_slice.85
  298.9 0.6 add_select_fusion.2
  299.5 13.1 %fusion.43 = (f32[512]{0:T(512)S(1)}, f32[512,8704]{1,0:T(8,128)}) fusion(bf16[8704,128]{1,0:T(8,128)(2,1)} %get-tuple-element.660, bf16[2,512,128]{2,1,0:T(8,128)(2,1)S(1)} %get-tuple-element.659, s32[]{:T(128)} %get-tuple-element.645, s32[8704]{0:T(1024)S(1)} %get-tuple-element.629, pred[8704]{0:T(1024)(128)(4,1)S(1)} %get-tuple-element.630, ...), kind=kOutput, calls=%fused_computation.80.clone.1 | convolution fusion | flops 1185414656 | bytes 20290564 | tf_op jit(solution)/shard_map/while/body/eval_jaxpr/while/body/eval_jaxpr/rd,kd->rk/dot_general | solution.py:51
  312.6 8.5 %fusion.44 = f32[512]{0:T(512)S(1)} fusion(f32[512,8704]{1,0:T(8,128)} %get-tuple-element.634, f32[512]{0:T(512)S(1)} %get-tuple-element.635), kind=kLoop, calls=%fused_computation.10.clone.1 | loop fusion | flops 8912384 | bytes 17829888 | tf_op jit(solution)/shard_map/while/body/eval_jaxpr/while/body/eval_jaxpr/reduce_sum | solution.py:58
  321.1 9.3 %fusion.45 = bf16[2,512,128]{2,1,0:T(8,128)(2,1)S(1)} fusion(bf16[2,512,128]{2,1,0:T(8,128)(2,1)S(1)} %get-tuple-element.646, s32[]{:T(128)} %get-tuple-element.645, bf16[8704,128]{1,0:T(8,128)(2,1)} %get-tuple-element.661, f32[512,8704]{1,0:T(8,128)} %get-tuple-element.634, f32[512]{0:T(512)S(1)} %get-tuple-element.635, f32[512]{0:T(512)S(1)} %fusion.44), kind=kOutput, calls=%fused_computation.17.clone.1 | convolution fusion | flops 1149894656 | bytes 20189188 | tf_op jit(solution)/shard_map/while/body/eval_jaxpr/while/body/eval_jaxpr/rk,kd->rd/dot_general | solution.py:59
  330.5 0.6 dynamic_slice.85
  331.1 0.6 add_select_fusion.2
  331.7 13.1 %fusion.43 = (f32[512]{0:T(512)S(1)}, f32[512,8704]{1,0:T(8,128)}) fusion(bf16[8704,128]{1,0:T(8,128)(2,1)} %get-tuple-element.660, bf16[2,512,128]{2,1,0:T(8,128)(2,1)S(1)} %get-tuple-element.659, s32[]{:T(128)} %get-tuple-element.645, s32[8704]{0:T(1024)S(1)} %get-tuple-element.629, pred[8704]{0:T(1024)(128)(4,1)S(1)} %get-tuple-element.630, ...), kind=kOutput, calls=%fused_computation.80.clone.1 | convolution fusion | flops 1185414656 | bytes 20290564 | tf_op jit(solution)/shard_map/while/body/eval_jaxpr/while/body/eval_jaxpr/rd,kd->rk/dot_general | solution.py:51
  344.8 8.5 %fusion.44 = f32[512]{0:T(512)S(1)} fusion(f32[512,8704]{1,0:T(8,128)} %get-tuple-element.634, f32[512]{0:T(512)S(1)} %get-tuple-element.635), kind=kLoop, calls=%fused_computation.10.clone.1 | loop fusion | flops 8912384 | bytes 17829888 | tf_op jit(solution)/shard_map/while/body/eval_jaxpr/while/body/eval_jaxpr/reduce_sum | solution.py:58
  353.3 9.3 %fusion.45 = bf16[2,512,128]{2,1,0:T(8,128)(2,1)S(1)} fusion(bf16[2,512,128]{2,1,0:T(8,128)(2,1)S(1)} %get-tuple-element.646, s32[]{:T(128)} %get-tuple-element.645, bf16[8704,128]{1,0:T(8,128)(2,1)} %get-tuple-element.661, f32[512,8704]{1,0:T(8,128)} %get-tuple-element.634, f32[512]{0:T(512)S(1)} %get-tuple-element.635, f32[512]{0:T(512)S(1)} %fusion.44), kind=kOutput, calls=%fused_computation.17.clone.1 | convolution fusion | flops 1149894656 | bytes 20189188 | tf_op jit(solution)/shard_map/while/body/eval_jaxpr/while/body/eval_jaxpr/rk,kd->rd/dot_general | solution.py:59
  362.7 0.8 copy-done.5
  363.5 1.0 copy-done.1
  (41 shorter events, 0.4 us)
Async XLA Ops:
  0.0 5.8 %copy-start = (bf16[2,4096,128]{2,1,0:T(8,128)(2,1)S(1)}, bf16[2,4096,128]{2,1,0:T(8,128)(2,1)}, u32[]{:S(2)}) copy-start(bf16[2,4096,128]{2,1,0:T(8,128)(2,1)} %param.20) | copy-start | bytes 6291460
  17.4 54.6 %all-to-all-start = ((bf16[4,2,4,256,128]{4,3,2,1,0:T(8,128)(2,1)}), bf16[4,2,4,256,128]{4,3,2,1,0:T(8,128)(2,1)S(1)}, u32[]{:S(2)}, u32[]{:S(2)}) async-start(bf16[4,2,4,256,128]{4,3,2,1,0:T(8,128)(2,1)} %pad_maximum_fusion.4), calls=%async_computation | async-start | bytes 4194304 | tf_op jit(solution)/shard_map/all_to_all | solution.py:112
  71.9 52.4 %all-to-all-start.1 = ((bf16[2,16,256,128]{3,2,0,1:T(8,128)(2,1)}), bf16[2,16,256,128]{3,2,0,1:T(8,128)(2,1)}, u32[]{:S(2)}, u32[]{:S(2)}) async-start(bf16[2,16,256,128]{3,2,0,1:T(8,128)(2,1)} %copy.21), calls=%async_computation.1 | async-start | bytes 4194304 | tf_op jit(solution)/shard_map/all_to_all | solution.py:117
  80.6 47.5 %copy-start.3 = (bf16[2,256,128]{2,1,0:T(8,128)(2,1)S(1)}, bf16[2,256,128]{2,1,0:T(8,128)(2,1)}, u32[]{:S(2)}) copy-start(bf16[2,256,128]{2,1,0:T(8,128)(2,1)} %param.18) | copy-start | bytes 393220
  80.6 51.4 %copy-start.4 = (bf16[2,256,128]{2,1,0:T(8,128)(2,1)S(1)}, bf16[2,256,128]{2,1,0:T(8,128)(2,1)}, u32[]{:S(2)}) copy-start(bf16[2,256,128]{2,1,0:T(8,128)(2,1)} %param.17) | copy-start | bytes 393220
  80.6 78.2 %collective-permute-start = (bf16[2,16,256,128]{3,2,1,0:T(8,128)(2,1)S(1)}, bf16[2,16,256,128]{3,2,1,0:T(8,128)(2,1)}, u32[]{:S(2)}, u32[]{:S(2)}) collective-permute-start(bf16[2,16,256,128]{3,2,1,0:T(8,128)(2,1)S(1)} %bitcast.69), channel_id=1, source_target_pairs={{0,4},{4,0},{8,12},{12,8},{1,5},{5,1},{9,13},{13,9},{2,6},{6,2},{1... | collective-permute-start | bytes 6291464 | tf_op jit(solution)/shard_map/ppermute | solution.py:28
  128.0 73.9 %collective-permute-start.2 = (bf16[2,16,256,128]{3,2,1,0:T(8,128)(2,1)}, bf16[2,16,256,128]{3,2,1,0:T(8,128)(2,1)}, u32[]{:S(2)}, u32[]{:S(2)}) collective-permute-start(bf16[2,16,256,128]{3,2,1,0:T(8,128)(2,1)} %bitcast.71), channel_id=1, source_target_pairs={{0,4},{4,0},{8,12},{12,8},{1,5},{5,1},{9,13},{13,9},{2,6},{6,2},{1... | collective-permute-start | bytes 6291464 | tf_op jit(solution)/shard_map/ppermute | solution.py:28
  128.1 77.5 %collective-permute-start.3 = (bf16[2,256,128]{2,1,0:T(8,128)(2,1)S(1)}, bf16[2,256,128]{2,1,0:T(8,128)(2,1)S(1)}, u32[]{:S(2)}, u32[]{:S(2)}) collective-permute-start(bf16[2,256,128]{2,1,0:T(8,128)(2,1)S(1)} %copy-done.3), channel_id=1, source_target_pairs={{0,4},{4,8},{8,12},{1,5},{5,9},{9,13},{2,6},{6,10},{10,14},{3,7},{... | collective-permute-start | bytes 393224 | tf_op jit(solution)/shard_map/ppermute | solution.py:14
  132.0 83.9 %collective-permute-start.1 = (bf16[2,256,128]{2,1,0:T(8,128)(2,1)S(1)}, bf16[2,256,128]{2,1,0:T(8,128)(2,1)S(1)}, u32[]{:S(2)}, u32[]{:S(2)}) collective-permute-start(bf16[2,256,128]{2,1,0:T(8,128)(2,1)S(1)} %copy-done.4), channel_id=1, source_target_pairs={{0,4},{4,8},{8,12},{1,5},{5,9},{9,13},{2,6},{6,10},{10,14},{3,7},{... | collective-permute-start | bytes 393224 | tf_op jit(solution)/shard_map/ppermute | solution.py:14
  215.9 9.9 %copy-start.2 = (bf16[8,256,128]{2,1,0:T(8,128)(2,1)S(1)}, bf16[8,256,128]{2,1,0:T(8,128)(2,1)}, u32[]{:S(2)}) copy-start(bf16[8,256,128]{2,1,0:T(8,128)(2,1)} %param.16) | copy-start | bytes 1572868
  362.7 0.8 copy-start.5
  362.7 1.8 copy-start.1
